TPU v7x, 32 devices: a whole 2x2x4 slice. The times are simulated.
32 devices in a mesh: groups: 2 (over y), blk: 4 (over z), split: 2 (over x), sub: 2 (over core).
Axes of the slice: x: 2, y: 2, z: 4, core: 2. Of those that a mesh axis runs over, the one named last changes fastest.
Arguments:
- attention_output_rows: bfloat16 [1024, 8192], P(('groups', 'blk'), 'split'), parts along dimension 0, may hold values from -6 to 6
- residual: bfloat16 [1024, 8192], P(('groups', 'split'), ('blk', 'sub')), parts along dimension 0, may hold values from -6 to 6
- output_projection_weight: bfloat16 [8192, 8192], P('split', ('blk', 'sub')), may hold values from -0.0625 to 0.0625
- down_adapter_bank: bfloat16 [4, 64, 8192], P('blk', None, 'split'), may hold values from -0.0625 to 0.0625
- up_adapter_bank: bfloat16 [4, 64, 8192], P('split', None, ('blk', 'sub')), may hold values from -0.75 to 0.75
- rollout_row_tenant: int32 [1024], P('groups'), parts along dimension 0, may hold values from 0 to 3, as said below
- tenant_bank_entry: int32 [4], replicated, may hold values from 0 to 3, each once
- tenant_live_rank: int32 [4], replicated, may hold values from 16 to 64, as said below
Outputs:
- layer_out: bfloat16 [1024, 8192], P(('groups', 'split'), ('blk', 'sub')), parts along dimension 0
There are 2 independent parts, one for each index of `groups`. A program takes and returns all parts, laid end to end along the dimension named above; an argument that names none is the same for every part. Nothing has to cross between parts.
Inputs may be any that keep to these rules, and one draw needn't show every extreme that they name: `rollout_row_tenant`: every tenant owns at least one row of every part. `tenant_live_rank`: some tenant has the full rank 64.
All inputs are finite; a program needn't handle non-finite values.
Results may differ from a plain program's by a relative error of at most 0.0038.
Values may be sent and summed in bfloat16 or wider, within the bound.
A program may use at most 64 MiB of HBM per device.

v0:
```python
import jax
import jax.numpy as jnp
from jax import lax
from jax.sharding import PartitionSpec as P


def shards(
    attention_output_rows,
    residual,
    output_projection_weight,
    down_adapter_bank,
    up_adapter_bank,
    rollout_row_tenant,
    tenant_bank_entry,
    tenant_live_rank,
):
    out_cols = output_projection_weight.shape[1]
    feat_width = attention_output_rows.shape[1]
    rank_mask_rows = down_adapter_bank.shape[1]
    gathered_down_maps = lax.all_gather(down_adapter_bank, "blk", axis=0, tiled=True)
    tenant_count = gathered_down_maps.shape[0]
    total_rows = rollout_row_tenant.shape[0]
    tenant_ids = jnp.arange(tenant_count, dtype=jnp.int32)
    tenant_hot = (rollout_row_tenant[:, None] == tenant_ids[None, :]).astype(jnp.int32)
    slot_all = jnp.sum(tenant_hot * tenant_bank_entry[None, :], axis=1)
    rank_all = jnp.sum(tenant_hot * tenant_live_rank[None, :], axis=1)
    down_cols = gathered_down_maps.reshape(tenant_count * rank_mask_rows, feat_width).T
    joined = jnp.concatenate([output_projection_weight, down_cols], axis=1)
    own_count = total_rows // lax.axis_size("split")
    own_start = lax.axis_index("split") * own_count
    own_slot = lax.dynamic_slice_in_dim(slot_all, own_start, own_count, 0)
    own_rank = lax.dynamic_slice_in_dim(rank_all, own_start, own_count, 0)
    own_hot = own_slot[:, None] == tenant_ids[None, :]
    full = jnp.dot(
        lax.all_gather(attention_output_rows, "blk", axis=0, tiled=True),
        joined,
        preferred_element_type=jnp.float32,
    )
    piece_hot = slot_all[:, None] == tenant_ids[None, :]
    values = full[:, out_cols:]
    shaped = values.reshape(values.shape[0], tenant_count, rank_mask_rows)
    products = jnp.concatenate(
        [
            full[:, :out_cols],
            jnp.sum(jnp.where(piece_hot[:, :, None], shaped, jnp.zeros((), jnp.float32)), axis=1),
        ],
        axis=1,
    )
    summed = lax.psum_scatter(products, "split", scatter_dimension=0, tiled=True)
    frozen_output_term = summed[:, :out_cols]
    low_rank = summed[:, out_cols:]
    gathered_up_maps = lax.all_gather(up_adapter_bank, "split", axis=0, tiled=True)
    kept_mask = jnp.arange(rank_mask_rows, dtype=jnp.int32)[None, :] < own_rank[:, None]
    scaling = rank_mask_rows / own_rank.astype(jnp.float32)
    low_scaled = jnp.where(
        kept_mask, low_rank * scaling[:, None], jnp.zeros((), jnp.float32)
    ).astype(jnp.bfloat16)
    rank_expanded_rows = jnp.where(
        own_hot[:, :, None], low_scaled[:, None, :], jnp.zeros((), jnp.bfloat16)
    ).reshape(own_count, tenant_count * rank_mask_rows)
    adapter_output_term = jnp.dot(
        rank_expanded_rows,
        gathered_up_maps.reshape(tenant_count * rank_mask_rows, out_cols),
        preferred_element_type=jnp.float32,
    )
    return (residual.astype(jnp.float32) + frozen_output_term + adapter_output_term).astype(
        jnp.bfloat16
    )


def solution(mesh):
    in_specs = (
        P(("groups", "blk"), "split"),
        P(("groups", "split"), ("blk", "sub")),
        P("split", ("blk", "sub")),
        P("blk", None, "split"),
        P("split", None, ("blk", "sub")),
        P("groups"),
        P(),
        P(),
    )
    out_specs = P(("groups", "split"), ("blk", "sub"))
    return jax.shard_map(shards, mesh=mesh, in_specs=in_specs, out_specs=out_specs, check_vma=False)
```

profile of v0, /device:TPU:0, one launch (start us, length us, event | category | flops | bytes accessed | tf_op | source)
XLA Modules:
  0.0 194.9 jit_solution(4081771632402627207)
XLA Ops:
  6.5 0.0 all-gather.3.cloned.1.call-start
  6.5 0.7 all-gather.3.cloned.1.call-update
  7.3 0.0 all-gather.5.cloned.1.call-start
  7.3 0.7 all-gather.5.cloned.1.call-update
  8.0 0.0 reduce-scatter.2.cloned.1.call-start
  8.1 0.8 select_reduce_fusion.1
  8.8 48.5 %all-gather.3.cloned.1.call-done = bf16[4,64,4096]{2,1,0:T(8,128)(2,1)} async-done(((bf16[1,64,4096]{2,1,0:T(8,128)(2,1)}), bf16[4,64,4096]{2,1,0:T(8,128)(2,1)}) %all-gather.3.cloned.1.call-update) | async-done | bytes 2097168 | tf_op jit(solution)/shard_map/all_gather | solution.py:20
  57.3 3.3 %copy.18 = bf16[256,4096]{0,1:T(8,128)(2,1)S(1)} copy(bf16[256,4096]{1,0:T(8,128)(2,1)} %bitcast.14) | data formatting | bytes 4194304 | tf_op jit(solution)/shard_map/reshape | solution.py:27
  60.6 77.9 %all-gather.5.cloned.1.call-done = bf16[512,4096]{1,0:T(8,128)(2,1)} async-done(((bf16[128,4096]{1,0:T(8,128)(2,1)}), bf16[512,4096]{1,0:T(8,128)(2,1)}) %all-gather.5.cloned.1.call-update) | async-done | bytes 4194320 | tf_op jit(solution)/shard_map/all_gather | solution.py:35
  138.5 9.7 %fusion.4 = f32[512,1280]{0,1:T(8,128)S(1)} fusion(bf16[512,4096]{1,0:T(8,128)(2,1)} %all-gather.5.cloned.1.call-done, bf16[4096,256]{1,0:T(8,128)(2,1)S(1)} %bitcast.15, bf16[4096,1024]{1,0:T(8,128)(2,1)} %param.10), kind=kOutput, calls=%fused_computation.4 | convolution fusion | flops 5389680640 | bytes 17301504 | tf_op jit(solution)/shard_map/dot_general | solution.py:34
  148.2 0.2 slice.16
  148.4 0.1 select_reduce_fusion
  148.5 0.0 copy-start
  148.5 1.6 pad_maximum_fusion
  150.0 0.0 copy-start.1
  150.0 0.0 reduce-scatter.2.cloned.1.call-update
  150.1 0.1 dynamic_slice.6
  150.1 0.0 copy-done
  150.1 0.2 copy.17
  150.4 0.1 convert_divide_fusion
  150.4 0.5 copy-done.1
  151.0 12.9 %all_gather.11 = bf16[4,64,1024]{2,1,0:T(8,128)(2,1)S(1)} all-gather(bf16[2,64,1024]{2,1,0:T(8,128)(2,1)S(1)} %copy-done.1), channel_id=1, replica_groups=mesh['groups'=2,'blk'=4,'split'=2,'sub'=2] {'split'}, dimensions={0}, use_global_device_ids=true | all-gather | bytes 786432 | tf_op jit(solution)/shard_map/all_gather | solution.py:52
  163.9 21.1 %reduce-scatter.2.cloned.1.call-done = f32[256,1088]{0,1:T(8,128)} async-done(((f32[512,1088]{0,1:T(8,128)}), f32[256,1088]{0,1:T(8,128)}) %reduce-scatter.2.cloned.1.call-update) | async-done | bytes 1114128 | tf_op jit(solution)/shard_map/reduce_scatter | solution.py:49
  185.0 0.9 fusion.12
  185.8 1.6 fusion.8
  187.4 1.0 copy.20
  (3 shorter events, 0.1 us)
Async XLA Ops:
  6.5 50.8 %all-gather.3.cloned.1.call-start = ((), (), s32[]{:S(2)}) async-start(), calls=%async_computation.1 | async-start | bytes 2621440 | tf_op jit(solution)/shard_map/all_gather | solution.py:20
  7.3 131.2 %all-gather.5.cloned.1.call-start = ((), (), s32[]{:S(2)}) async-start(), calls=%async_computation.2 | async-start | bytes 5242880 | tf_op jit(solution)/shard_map/all_gather | solution.py:35
  8.0 177.0 %reduce-scatter.2.cloned.1.call-start = ((), (), s32[]{:S(2)}) async-start(), calls=%async_computation.3 | async-start | bytes 3342336 | tf_op jit(solution)/shard_map/reduce_scatter | solution.py:49
  148.5 1.7 copy-start
  150.0 0.9 copy-start.1
Sparse Core Ops, SparseCore 0:
  8.9 48.3 all-gather.2
  58.9 79.5 all-gather.4
  150.2 34.7 reduce-scatter.1
where the time goes:
time: 195 us
  waiting for transfers between devices  149 us (76%)
  between operations  13.2 us (7%)
  blocking collectives  12.9 us (7%)
  matrix products  11.3 us (6%)
  local copies, waits for them, and re-layouts  5.31 us (3%)
  other arithmetic  3.35 us (2%)
    all_gather x1, waiting for transfers between devices, shards(): lax.all_gather(attention_output_rows, 'blk', axis=0, tiled=True)  77.9 us
    all_gather x1, waiting for transfers between devices, shards(): lax.all_gather(down_adapter_bank, 'blk', axis=0, tiled=True)  48.5 us
    reduce_scatter x1, waiting for transfers between devices, shards(): lax.psum_scatter(products, 'split', scatter_dimension=0, tiled=True)  21.1 us
    all_gather x1, blocking collectives, shards(): lax.all_gather(up_adapter_bank, 'split', axis=0, tiled=True)  12.9 us
    dot_general x1, matrix products, shards(): jnp.dot(lax.all_gather(attention_output_rows, 'blk', axis=0, tiled=True),...  9.71 us
  transfers between devices with their start and end apart: 3, of which 3 were waited for; matrix products, arithmetic and copies ran while one was open for 2% of the time, Pallas kernels for 0%

commit v1 on v0

--- a/solution.py
+++ b/solution.py
@@ -17,7 +17,12 @@
     out_cols = output_projection_weight.shape[1]
     feat_width = attention_output_rows.shape[1]
     rank_mask_rows = down_adapter_bank.shape[1]
-    gathered_down_maps = lax.all_gather(down_adapter_bank, "blk", axis=0, tiled=True)
+    ring = [down_adapter_bank]
+    for hop in range(3):
+        ring.append(lax.ppermute(ring[-1], "blk", [(dev, (dev + 1) % 4) for dev in range(4)]))
+    gathered_down_maps = jnp.roll(
+        jnp.concatenate(ring[::-1], axis=0), (lax.axis_index("blk") + 1) * ring[0].shape[0], axis=0
+    )
     tenant_count = gathered_down_maps.shape[0]
     total_rows = rollout_row_tenant.shape[0]
     tenant_ids = jnp.arange(tenant_count, dtype=jnp.int32)

time: 195 us -> 172 us (0.88)
  waiting for transfers between devices: 149 us -> 108 us
  starting transfers between devices: 0.08 us -> 18.9 us
    ppermute x0 -> x3, waiting for transfers between devices: none -> 62.9 us  [shards(): lax.ppermute(ring[-1], 'blk', [(dev, (dev + 1) % 4) for dev in range(4)])]
    all_gather x1, waiting for transfers between devices: 77.9 us -> 22.3 us  [shards(): lax.all_gather(attention_output_rows, 'blk', axis=0, tiled=True)]
    all_gather x1 -> x0, waiting for transfers between devices: 48.5 us -> none  [shards(): lax.all_gather(down_adapter_bank, 'blk', axis=0, tiled=True)]
    ppermute x0 -> x3, starting transfers between devices: none -> 18.8 us  [shards(): lax.ppermute(ring[-1], 'blk', [(dev, (dev + 1) % 4) for dev in range(4)])]
    reshape x1 -> x0, local copies, waits for them, and re-layouts: 3.27 us -> none  [shards(): gathered_down_maps.reshape(tenant_count * rank_mask_rows, feat_width)]
    transpose x0 -> x1, local copies, waits for them, and re-layouts: none -> 2.47 us  [shards(): gathered_down_maps.reshape(tenant_count * rank_mask_rows, feat_width)]
  transfers between devices with their start and end apart: 3 -> 5, of which waited for: 3 -> 5; matrix products, arithmetic and copies ran while one was open for 2% -> 2% of each run, Pallas kernels for 0% -> 0%
where the time goes in v1:
time: 172 us
  waiting for transfers between devices  108 us (63%)
  starting transfers between devices  18.9 us (11%)
  between operations  13.6 us (8%)
  blocking collectives  12.1 us (7%)
  matrix products  11.2 us (7%)
  local copies, waits for them, and re-layouts  4.41 us (3%)
  other arithmetic  3.34 us (2%)
    ppermute x3, waiting for transfers between devices, shards(): lax.ppermute(ring[-1], 'blk', [(dev, (dev + 1) % 4) for dev in range(4)])  62.9 us
    all_gather x1, waiting for transfers between devices, shards(): lax.all_gather(attention_output_rows, 'blk', axis=0, tiled=True)  22.3 us
    reduce_scatter x1, waiting for transfers between devices, shards(): lax.psum_scatter(products, 'split', scatter_dimension=0, tiled=True)  22.2 us
    ppermute x3, starting transfers between devices, shards(): lax.ppermute(ring[-1], 'blk', [(dev, (dev + 1) % 4) for dev in range(4)])  18.8 us
    all_gather x1, blocking collectives, shards(): lax.all_gather(up_adapter_bank, 'split', axis=0, tiled=True)  12.1 us
    dot_general x1, matrix products, shards(): jnp.dot(lax.all_gather(attention_output_rows, 'blk', axis=0, tiled=True),...  9.64 us
  transfers between devices with their start and end apart: 5, of which 5 were waited for; matrix products, arithmetic and copies ran while one was open for 2% of the time, Pallas kernels for 0%

profile of v1, /device:TPU:0, one launch (start us, length us, event | category | flops | bytes accessed | tf_op | source)
XLA Modules:
  0.0 171.6 jit_solution(5337059086509351239)
XLA Ops:
  6.5 0.0 copy-start
  6.5 0.0 all-gather.2.cloned.1.call-start
  6.5 0.7 all-gather.2.cloned.1.call-update
  7.3 0.0 reduce-scatter.2.cloned.1.call-start
  7.3 3.1 %collective-permute-start = (bf16[1,64,4096]{2,1,0:T(8,128)(2,1)}, bf16[1,64,4096]{2,1,0:T(8,128)(2,1)S(1)}, u32[]{:S(2)}, u32[]{:S(2)}) collective-permute-start(bf16[1,64,4096]{2,1,0:T(8,128)(2,1)} %param.11), channel_id=1, source_target_pairs={{0,4},{4,8},{8,12},{12,0},{1,5},{5,9},{9,13},{13,1},{2,6},{6,10},{... | collective-permute-start | bytes 1572872 | tf_op jit(solution)/shard_map/ppermute | solution.py:22
  10.4 14.4 %collective-permute-done = bf16[1,64,4096]{2,1,0:T(8,128)(2,1)S(1)} collective-permute-done((bf16[1,64,4096]{2,1,0:T(8,128)(2,1)}, bf16[1,64,4096]{2,1,0:T(8,128)(2,1)S(1)}, u32[]{:S(2)}, u32[]{:S(2)}) %collective-permute-start) | collective-permute-done | bytes 524320 | tf_op jit(solution)/shard_map/ppermute | solution.py:22
  24.8 4.5 %collective-permute-start.1 = (bf16[1,64,4096]{2,1,0:T(8,128)(2,1)S(1)}, bf16[1,64,4096]{2,1,0:T(8,128)(2,1)S(1)}, u32[]{:S(2)}, u32[]{:S(2)}) collective-permute-start(bf16[1,64,4096]{2,1,0:T(8,128)(2,1)S(1)} %collective-permute-done), channel_id=1, source_target_pairs={{0,4},{4,8},{8,12},{12,0},{1,5},{5,9},{9,13},{13,1},{2,6},{6,10},{... | collective-permute-start | bytes 1572872 | tf_op jit(solution)/shard_map/ppermute | solution.py:22
  29.3 24.0 %collective-permute-done.1 = bf16[1,64,4096]{2,1,0:T(8,128)(2,1)S(1)} collective-permute-done((bf16[1,64,4096]{2,1,0:T(8,128)(2,1)S(1)}, bf16[1,64,4096]{2,1,0:T(8,128)(2,1)S(1)}, u32[]{:S(2)}, u32[]{:S(2)}) %collective-permute-start.1) | collective-permute-done | bytes 524320 | tf_op jit(solution)/shard_map/ppermute | solution.py:22
  53.3 11.2 %collective-permute-start.2 = (bf16[1,64,4096]{2,1,0:T(8,128)(2,1)S(1)}, bf16[1,64,4096]{2,1,0:T(8,128)(2,1)S(1)}, u32[]{:S(2)}, u32[]{:S(2)}) collective-permute-start(bf16[1,64,4096]{2,1,0:T(8,128)(2,1)S(1)} %collective-permute-done.1), channel_id=1, source_target_pairs={{0,4},{4,8},{8,12},{12,0},{1,5},{5,9},{9,13},{13,1},{2,6},{6,10},{... | collective-permute-start | bytes 1572872 | tf_op jit(solution)/shard_map/ppermute | solution.py:22
  64.6 0.8 select_reduce_fusion.1
  65.3 24.5 %collective-permute-done.2 = bf16[1,64,4096]{2,1,0:T(8,128)(2,1)S(1)} collective-permute-done((bf16[1,64,4096]{2,1,0:T(8,128)(2,1)S(1)}, bf16[1,64,4096]{2,1,0:T(8,128)(2,1)S(1)}, u32[]{:S(2)}, u32[]{:S(2)}) %collective-permute-start.2) | collective-permute-done | bytes 524320 | tf_op jit(solution)/shard_map/ppermute | solution.py:22
  90.0 0.0 copy-done
  90.2 0.1 constant_dynamic-slice_fusion
  90.4 2.5 %copy.21 = bf16[4096,256]{1,0:T(8,128)(2,1)} copy(bf16[4096,256]{0,1:T(8,128)(2,1)S(1)} %bitcast.14) | data formatting | bytes 4194304 | tf_op jit(solution)/shard_map/transpose | solution.py:32
  92.8 22.3 %all-gather.2.cloned.1.call-done = bf16[512,4096]{1,0:T(8,128)(2,1)} async-done(((bf16[128,4096]{1,0:T(8,128)(2,1)}), bf16[512,4096]{1,0:T(8,128)(2,1)}) %all-gather.2.cloned.1.call-update) | async-done | bytes 4194320 | tf_op jit(solution)/shard_map/all_gather | solution.py:40
  115.1 9.6 %fusion.4 = f32[512,1280]{0,1:T(8,128)S(1)} fusion(bf16[512,4096]{1,0:T(8,128)(2,1)} %all-gather.2.cloned.1.call-done, bf16[4096,256]{1,0:T(8,128)(2,1)} %copy.21, bf16[4096,1024]{1,0:T(8,128)(2,1)} %param.10), kind=kOutput, calls=%fused_computation.4 | convolution fusion | flops 5389680640 | bytes 17301504 | tf_op jit(solution)/shard_map/dot_general | solution.py:39
  124.7 0.2 slice.16
  124.9 0.0 copy-start.1
  125.0 0.0 copy-start.2
  125.0 0.1 select_reduce_fusion
  125.1 1.6 pad_maximum_fusion
  126.6 0.0 reduce-scatter.2.cloned.1.call-update
  126.6 0.1 dynamic_slice.11
  126.7 0.0 copy-done.1
  126.7 0.2 copy.20
  126.9 0.1 convert_divide_fusion
  127.0 0.0 copy-done.2
  127.0 12.1 %all_gather.7 = bf16[4,64,1024]{2,1,0:T(8,128)(2,1)S(1)} all-gather(bf16[2,64,1024]{2,1,0:T(8,128)(2,1)S(1)} %copy-done.2), channel_id=1, replica_groups=mesh['groups'=2,'blk'=4,'split'=2,'sub'=2] {'split'}, dimensions={0}, use_global_device_ids=true | all-gather | bytes 786432 | tf_op jit(solution)/shard_map/all_gather | solution.py:57
  139.1 22.2 %reduce-scatter.2.cloned.1.call-done = f32[256,1088]{0,1:T(8,128)} async-done(((f32[512,1088]{0,1:T(8,128)}), f32[256,1088]{0,1:T(8,128)}) %reduce-scatter.2.cloned.1.call-update) | async-done | bytes 1114128 | tf_op jit(solution)/shard_map/reduce_scatter | solution.py:54
  161.3 0.9 fusion.12
  162.2 1.6 fusion.8
  163.7 1.0 copy.23
  (11 shorter events, 0.3 us)
Async XLA Ops:
  6.5 83.4 %copy-start = (bf16[1,64,4096]{2,1,0:T(8,128)(2,1)S(1)}, bf16[1,64,4096]{2,1,0:T(8,128)(2,1)}, u32[]{:S(2)}) copy-start(bf16[1,64,4096]{2,1,0:T(8,128)(2,1)} %param.11) | copy-start | bytes 1572868
  6.5 108.6 %all-gather.2.cloned.1.call-start = ((), (), s32[]{:S(2)}) async-start(), calls=%async_computation.1 | async-start | bytes 5242880 | tf_op jit(solution)/shard_map/all_gather | solution.py:40
  7.3 154.1 %reduce-scatter.2.cloned.1.call-start = ((), (), s32[]{:S(2)}) async-start(), calls=%async_computation.2 | async-start | bytes 3342336 | tf_op jit(solution)/shard_map/reduce_scatter | solution.py:54
  7.3 17.5 %collective-permute-start = (bf16[1,64,4096]{2,1,0:T(8,128)(2,1)}, bf16[1,64,4096]{2,1,0:T(8,128)(2,1)S(1)}, u32[]{:S(2)}, u32[]{:S(2)}) collective-permute-start(bf16[1,64,4096]{2,1,0:T(8,128)(2,1)} %param.11), channel_id=1, source_target_pairs={{0,4},{4,8},{8,12},{12,0},{1,5},{5,9},{9,13},{13,1},{2,6},{6,10},{... | collective-permute-start | bytes 1572872 | tf_op jit(solution)/shard_map/ppermute | solution.py:22
  24.8 28.5 %collective-permute-start.1 = (bf16[1,64,4096]{2,1,0:T(8,128)(2,1)S(1)}, bf16[1,64,4096]{2,1,0:T(8,128)(2,1)S(1)}, u32[]{:S(2)}, u32[]{:S(2)}) collective-permute-start(bf16[1,64,4096]{2,1,0:T(8,128)(2,1)S(1)} %collective-permute-done), channel_id=1, source_target_pairs={{0,4},{4,8},{8,12},{12,0},{1,5},{5,9},{9,13},{13,1},{2,6},{6,10},{... | collective-permute-start | bytes 1572872 | tf_op jit(solution)/shard_map/ppermute | solution.py:22
  53.3 36.5 %collective-permute-start.2 = (bf16[1,64,4096]{2,1,0:T(8,128)(2,1)S(1)}, bf16[1,64,4096]{2,1,0:T(8,128)(2,1)S(1)}, u32[]{:S(2)}, u32[]{:S(2)}) collective-permute-start(bf16[1,64,4096]{2,1,0:T(8,128)(2,1)S(1)} %collective-permute-done.1), channel_id=1, source_target_pairs={{0,4},{4,8},{8,12},{12,0},{1,5},{5,9},{9,13},{13,1},{2,6},{6,10},{... | collective-permute-start | bytes 1572872 | tf_op jit(solution)/shard_map/ppermute | solution.py:22
  124.9 1.8 %copy-start.1 = (bf16[256,1024]{1,0:T(8,128)(2,1)S(1)}, bf16[256,1024]{1,0:T(8,128)(2,1)}, u32[]{:S(2)}) copy-start(bf16[256,1024]{1,0:T(8,128)(2,1)} %param.9) | copy-start | bytes 1572868
  125.0 2.0 %copy-start.2 = (bf16[2,64,1024]{2,1,0:T(8,128)(2,1)S(1)}, bf16[2,64,1024]{2,1,0:T(8,128)(2,1)}, u32[]{:S(2)}) copy-start(bf16[2,64,1024]{2,1,0:T(8,128)(2,1)} %param.12) | copy-start | bytes 786436
Sparse Core Ops, SparseCore 0:
  8.9 106.1 all-gather.1
  126.8 34.5 reduce-scatter.1
